TPU v7x, 256 devices: a whole 4x4x8 slice. The times are simulated.
256 devices in a mesh: narrow: 16 (over z, core), wide: 16 (over x, y).
Axes of the slice: x: 4, y: 4, z: 8, core: 2. Of those that a mesh axis runs over, the one named last changes fastest.
Arguments:
- inputs: bfloat16 [2048, 8192], P('narrow', 'wide'), may hold values from -6 to 6
- gate_blocks: bfloat16 [112, 16, 128, 128], P('wide', 'narrow'), may hold values from -0.125 to 0.125
- up_blocks: bfloat16 [112, 16, 128, 128], P('wide', 'narrow'), may hold values from -0.125 to 0.125
- pattern: int32 [112, 16], P('wide'), may hold values from 0 to 63, as said below
- grad_hidden: bfloat16 [2048, 14336], P('narrow', 'wide'), may hold values from -0.59765625 to 0.59765625
Outputs:
- hidden: bfloat16 [2048, 14336], P('narrow', 'wide')
- grad_inputs: bfloat16 [2048, 8192], P('narrow', 'wide')
- grad_gate: bfloat16 [112, 16, 128, 128], P('wide', 'narrow')
- grad_up: bfloat16 [112, 16, 128, 128], P('wide', 'narrow')
Inputs may be any that keep to these rules, and one draw needn't show every extreme that they name: pattern[j, k] = b_j XOR m_k, with one offset b_j for each block column and 16 distinct masks m_k common to all block columns, so each block column lists 16 distinct block rows.
All inputs are finite; a program needn't handle non-finite values.
Results may differ from a plain program's by a relative error of at most 0.023.
Values may be sent and summed in bfloat16 or wider, within the bound.
A program may use at most 128 MiB of HBM per device.

v0:
```python
import jax
import jax.numpy as jnp
from jax import lax
from jax.sharding import PartitionSpec as P


def silu_parts(gate_sum):
    sigmoid_value = jax.nn.sigmoid(gate_sum)
    return (gate_sum * sigmoid_value, sigmoid_value * (1.0 + gate_sum * (1.0 - sigmoid_value)))


def shards(inputs, gate_blocks, up_blocks, pattern, grad_hidden):
    tokens_here = inputs.shape[0]
    block_size = gate_blocks.shape[2]
    columns = gate_blocks.shape[0]
    full_inputs = lax.all_gather(inputs, "wide", axis=1, tiled=True)
    row_blocks = full_inputs.shape[1] // block_size
    input_blocks = full_inputs.reshape(tokens_here, row_blocks, block_size)

    def picks_for():
        return jnp.take(input_blocks, pattern, axis=1)

    gate_all, up_all = (
        lax.all_gather(gate_blocks, "narrow", axis=1, tiled=True),
        lax.all_gather(up_blocks, "narrow", axis=1, tiled=True),
    )
    pieces = (gate_all, up_all)
    picked = picks_for()
    gate_sum = jnp.einsum("tjkb,jkbc->tjc", picked, pieces[0], preferred_element_type=jnp.float32)
    up_sum = jnp.einsum("tjkb,jkbc->tjc", picked, pieces[1], preferred_element_type=jnp.float32)
    gate_sum, up_sum = (gate_sum, up_sum)
    activation, derivative = silu_parts(gate_sum)
    hidden = (activation * up_sum).astype(jnp.bfloat16)
    cotangent = grad_hidden.reshape(tokens_here, columns, block_size).astype(jnp.float32)
    d_gate = (cotangent * up_sum * derivative).astype(jnp.bfloat16)
    d_up = (cotangent * activation).astype(jnp.bfloat16)
    zero_inputs = jnp.zeros((tokens_here, row_blocks, block_size), jnp.float32)
    pieces = (gate_all, up_all)
    number_slots = pieces[0].shape[1]

    def one_slot(k, running):
        gate_slot = lax.dynamic_index_in_dim(pieces[0], k, 1, keepdims=False)
        up_slot = lax.dynamic_index_in_dim(pieces[1], k, 1, keepdims=False)
        contribution = jnp.einsum(
            "tjc,jbc->tjb", d_gate, gate_slot, preferred_element_type=jnp.float32
        )
        contribution = contribution + jnp.einsum(
            "tjc,jbc->tjb", d_up, up_slot, preferred_element_type=jnp.float32
        )
        targets = lax.dynamic_index_in_dim(pattern, k, 1, keepdims=False)
        return running.at[:, targets].add(contribution)

    partial_inputs = lax.fori_loop(0, number_slots, one_slot, zero_inputs)
    grad_inputs = lax.psum_scatter(
        partial_inputs.reshape(tokens_here, row_blocks * block_size).astype(jnp.bfloat16),
        "wide",
        scatter_dimension=1,
        tiled=True,
    )
    picked_all = picks_for()
    gate_terms = jnp.einsum(
        "tjkb,tjc->jkbc", picked_all, d_gate, preferred_element_type=jnp.float32
    )
    up_terms = jnp.einsum("tjkb,tjc->jkbc", picked_all, d_up, preferred_element_type=jnp.float32)
    grad_gate, grad_up = (
        lax.psum_scatter(
            gate_terms.astype(jnp.bfloat16), "narrow", scatter_dimension=1, tiled=True
        ).astype(jnp.float32),
        lax.psum_scatter(
            up_terms.astype(jnp.bfloat16), "narrow", scatter_dimension=1, tiled=True
        ).astype(jnp.float32),
    )
    return (
        hidden.reshape(tokens_here, columns * block_size),
        grad_inputs,
        grad_gate.astype(jnp.bfloat16),
        grad_up.astype(jnp.bfloat16),
    )


def solution(mesh):
    placed = (
        P("narrow", "wide"),
        P("wide", "narrow", None, None),
        P("wide", "narrow", None, None),
        P("wide", None),
        P("narrow", "wide"),
    )
    return jax.shard_map(
        shards,
        mesh=mesh,
        in_specs=placed,
        out_specs=(
            P("narrow", "wide"),
            P("narrow", "wide"),
            P("wide", "narrow", None, None),
            P("wide", "narrow", None, None),
        ),
        check_vma=False,
    )
```

profile of v0, /device:TPU:32, one launch (start us, length us, event | category | flops | bytes accessed | tf_op | source)
XLA Modules:
  0.0 384.9 jit_solution(9591232748475014344)
XLA Ops:
  7.2 1.7 copy.60
  8.9 1.8 copy.65
  10.8 1.8 copy.63
  16.0 47.6 %all-gather.4.cloned.1.call-done = bf16[128,8192]{0,1:T(8,128)(2,1)} async-done(((bf16[128,512]{0,1:T(8,128)(2,1)}), bf16[128,8192]{0,1:T(8,128)(2,1)}) %all-gather.4.cloned.1.call-update) | async-done | bytes 2097168 | tf_op jit(solution)/shard_map/all_gather | solution.py:16
  63.6 3.2 copy.61
  66.8 3.0 gather_fusion
  69.8 6.1 %copy.62 = bf16[7,16,128,128]{2,3,1,0:T(8,128)(2,1)} copy(bf16[7,16,128,128]{3,2,1,0:T(8,128)(2,1)} %bitcast.89) | data formatting | bytes 7340032 | tf_op jit(solution)/shard_map/jit(_take)/gather | solution.py:21
  75.9 31.0 %all-gather.8.cloned.1.call-done = bf16[7,16,128,128]{2,3,1,0:T(8,128)(2,1)} async-done(((bf16[7,1,128,128]{2,3,1,0:T(8,128)(2,1)}), bf16[7,16,128,128]{2,3,1,0:T(8,128)(2,1)}) %all-gather.8.cloned.1.call-update) | async-done | bytes 3670032 | tf_op jit(solution)/shard_map/all_gather | solution.py:25
  106.9 4.4 %fusion.27 = f32[128,7,128]{0,2,1:T(8,128)S(1)} fusion(bf16[7,16,128,128]{2,3,1,0:T(8,128)(2,1)} %all-gather.8.cloned.1.call-done, bf16[7,16,128,128]{2,3,1,0:T(8,128)(2,1)} %copy.62, pred[7,16]{1,0:T(8,128)(4,1)S(1)} %compare_and_fusion), kind=kOutput, calls=%fused_computation.31 | convolution fusion | flops 471597056 | bytes 7798896 | tf_op jit(solution)/shard_map/tjkb,jkbc->tjc/dot_general | solution.py:30
  111.3 38.3 %all-gather.6.cloned.1.call-done = bf16[7,16,128,128]{2,3,1,0:T(8,128)(2,1)} async-done(((bf16[7,1,128,128]{2,3,1,0:T(8,128)(2,1)}), bf16[7,16,128,128]{2,3,1,0:T(8,128)(2,1)}) %all-gather.6.cloned.1.call-update) | async-done | bytes 3670032 | tf_op jit(solution)/shard_map/all_gather | solution.py:24
  149.6 4.5 %multiply_convert_fusion = (bf16[128,7,128]{0,2,1:T(8,128)(2,1)S(1)}, bf16[128,7,128]{0,2,1:T(8,128)(2,1)S(1)}, bf16[128,7,128]{0,2,1:T(8,128)(2,1)S(1)}) fusion(f32[128,7,128]{0,2,1:T(8,128)S(1)} %bitcast.91, f32[128,7,128]{0,2,1:T(8,128)S(1)} %fusion.27, bf16[7,16,128,128]{2,3,1,0:T(8,128)(2,1)} %all-gather.6.cloned.1.call-done, ...), kind=kOutput, calls=%fused_computation.33 | convolution fusion | flops 473317376 | bytes 8945776 | tf_op jit(solution)/shard_map/tjkb,jkbc->tjc/dot_general | solution.py:29
  154.3 5.1 %fusion.17 = bf16[7,16,128,128]{3,2,1,0:T(8,128)(2,1)} fusion(bf16[7,16,128,128]{2,3,1,0:T(8,128)(2,1)} %copy.62, pred[7,16]{1,0:T(8,128)(4,1)S(1)} %compare_and_fusion, bf16[128,7,128]{0,2,1:T(8,128)(2,1)S(1)} %get-tuple-element.191), kind=kOutput, calls=%fused_computation.23 | convolution fusion | flops 473432064 | bytes 7569520 | tf_op jit(solution)/shard_map/tjkb,tjc->jkbc/dot_general | solution.py:61
  159.6 5.0 %fusion.20 = bf16[7,16,128,128]{3,2,1,0:T(8,128)(2,1)} fusion(bf16[7,16,128,128]{2,3,1,0:T(8,128)(2,1)} %copy.62, pred[7,16]{1,0:T(8,128)(4,1)S(1)} %compare_and_fusion, bf16[128,7,128]{0,2,1:T(8,128)(2,1)S(1)} %get-tuple-element.190), kind=kOutput, calls=%fused_computation.24 | convolution fusion | flops 473432064 | bytes 7569520 | tf_op jit(solution)/shard_map/tjkb,tjc->jkbc/dot_general | solution.py:64
  164.7 2.5 broadcast_in_dim.15
  167.1 86.0 %while.13 = (s32[]{:T(128)}, f32[128,64,128]{2,0,1:T(8,128)}, s32[7,16]{0,1:T(8,128)S(1)}, bf16[7,16,128,128]{2,3,1,0:T(8,128)(2,1)}, bf16[128,7,128]{2,0,1:T(8,...) while((s32[]{:T(128)}, f32[128,64,128]{2,0,1:T(8,128)}, ...), condition=%wide.region_2.4_spmd, body=%wide.region_0.3_spmd.sunk | while | flops 58949656 | bytes 4587709 | solution.py:53
  167.2 1.2 fusion.56
  168.4 1.3 fusion.57
  169.9 2.6 scatter_fusion
  173.7 1.3 fusion.57
  175.2 2.7 scatter_fusion
  177.9 1.2 fusion.56
  179.2 1.3 fusion.57
  180.6 2.7 scatter_fusion
  183.3 1.2 fusion.56
  184.5 1.3 fusion.57
  186.0 2.7 scatter_fusion
  188.7 1.3 fusion.56
  189.9 1.3 fusion.57
  191.4 2.7 scatter_fusion
  195.3 1.3 fusion.57
  196.8 2.7 scatter_fusion
  199.4 1.3 fusion.56
  200.7 1.3 fusion.57
  202.1 2.7 scatter_fusion
  204.8 1.2 fusion.56
  206.1 1.3 fusion.57
  207.5 2.7 scatter_fusion
  210.2 1.2 fusion.56
  211.4 1.3 fusion.57
  212.9 2.6 scatter_fusion
  215.6 1.2 fusion.56
  216.8 1.3 fusion.57
  218.3 2.6 scatter_fusion
  220.9 1.3 fusion.56
  222.2 1.3 fusion.57
  223.6 2.6 scatter_fusion
  226.3 1.3 fusion.56
  227.5 1.3 fusion.57
  229.0 2.6 scatter_fusion
  232.9 1.3 fusion.57
  234.3 2.6 scatter_fusion
  237.0 1.2 fusion.56
  238.2 1.3 fusion.57
  239.7 2.7 scatter_fusion
  242.4 1.3 fusion.56
  243.6 1.3 fusion.57
  245.1 2.7 scatter_fusion
  247.8 1.2 fusion.56
  249.0 1.3 fusion.57
  250.5 2.7 scatter_fusion
  253.1 3.9 %copy_bitcast_fusion = bf16[128,8192]{1,0:T(8,128)(2,1)} fusion(f32[128,64,128]{2,0,1:T(8,128)} %get-tuple-element.129), kind=kLoop, calls=%fused_computation.25 | loop fusion | flops 1048576 | bytes 6291456 | tf_op jit(solution)/shard_map/convert_element_type | solution.py:55
  258.5 34.1 %all-reduce.5.cloned.1.call-done = (bf16[7,16,128,128]{3,2,1,0:T(8,128)(2,1)}, bf16[7,16,128,128]{3,2,1,0:T(8,128)(2,1)}) async-done(((bf16[7,16,128,128]{3,2,1,0:T(8,128)(2,1)}, bf16[7,16,128,128]{3,2,1,0:T(8,128)(2,1)}), (bf16[7,16,128,128]{3,2,1,0:T(8,128)(2,1)}, bf16[7,16,128,128]{3,2,1,0:T(8,128)(2,1)})) %all-reduce.5.cloned.1.call-update) | async-done | bytes 7340048
  292.6 2.5 constant_dynamic-slice_fusion.1
  295.1 83.3 %reduce-scatter.8.cloned.1.call-done = bf16[128,512]{1,0:T(8,128)(2,1)} async-done(((bf16[128,8192]{1,0:T(8,128)(2,1)}), bf16[128,512]{1,0:T(8,128)(2,1)}) %reduce-scatter.8.cloned.1.call-update) | async-done | bytes 131088 | tf_op jit(solution)/shard_map/reduce_scatter | solution.py:54
  (57 shorter events, 12.4 us)
Async XLA Ops:
  7.2 56.4 %all-gather.4.cloned.1.call-start = ((), (), s32[]{:S(2)}) async-start(), calls=%async_computation.1 | async-start | bytes 2228224 | tf_op jit(solution)/shard_map/all_gather | solution.py:16
  8.9 98.0 %all-gather.8.cloned.1.call-start = ((), (), s32[]{:S(2)}) async-start(), calls=%async_computation.3 | async-start | bytes 3899392 | tf_op jit(solution)/shard_map/all_gather | solution.py:25
  10.7 138.8 %all-gather.6.cloned.1.call-start = ((), (), s32[]{:S(2)}) async-start(), calls=%async_computation.2 | async-start | bytes 3899392 | tf_op jit(solution)/shard_map/all_gather | solution.py:24
  12.6 280.0 %all-reduce.5.cloned.1.call-start = ((), (), s32[]{:S(2)}) async-start(), calls=%async_computation.5 | async-start | bytes 14680064
  164.6 213.7 %reduce-scatter.8.cloned.1.call-start = ((), (), s32[]{:S(2)}) async-start(), calls=%async_computation.4 | async-start | bytes 2228224 | tf_op jit(solution)/shard_map/reduce_scatter | solution.py:54
  253.1 3.9 %copy-start = (u32[256]{0:T(256)S(1)}, u32[256]{0:T(256)}, u32[]{:S(2)}) copy-start(u32[256]{0:T(256)} %constant.58) | copy-start | bytes 3076
Sparse Core Ops, SparseCore 0:
  11.0 52.5 all-gather.3
  66.0 40.8 all-gather.7
  109.3 40.2 all-gather.5
  164.7 127.8 all-reduce.4
  296.6 81.7 reduce-scatter.7
where the time goes:
time: 387 us; the launch traced here: 385 us
  waiting for transfers between devices  234 us (60%)
  matrix products  59.2 us (15%)
  other arithmetic  47.8 us (12%)
  local copies, waits for them, and re-layouts  29.3 us (8%)
  between operations  13.8 us (4%)
    reduce_scatter x1, waiting for transfers between devices, shards(): lax.psum_scatter(partial_inputs.reshape(tokens_here, row_blocks * block_s...  83.3 us
    all_gather x1, waiting for transfers between devices, shards(): full_inputs = lax.all_gather(inputs, 'wide', axis=1, tiled=True)  47.6 us
    scatter-add x16, other arithmetic, one_slot(): return running.at[:, targets].add(contribution)  42.4 us
    all_gather x1, waiting for transfers between devices, shards(): lax.all_gather(gate_blocks, 'narrow', axis=1, tiled=True)  38.3 us
    unnamed x6, waiting for transfers between devices  34.2 us
    all_gather x1, waiting for transfers between devices, shards(): lax.all_gather(up_blocks, 'narrow', axis=1, tiled=True)  31 us
    dot_general x16, matrix products, one_slot(): jnp.einsum('tjc,jbc->tjb', d_up, up_slot, preferred_element_type=jnp.floa...  20.2 us
    dot_general x16, matrix products, one_slot(): jnp.einsum('tjc,jbc->tjb', d_gate, gate_slot, preferred_element_type=jnp....  20 us
  transfers between devices with their start and end apart: 5, of which 5 were waited for; matrix products, arithmetic and copies ran while one was open for 31% of the time, Pallas kernels for 0%

commit v1 on v0

--- a/solution.py
+++ b/solution.py
@@ -2,6 +2,28 @@
 import jax.numpy as jnp
 from jax import lax
 from jax.sharding import PartitionSpec as P
+
+
+def laid_out(tiles, dim):
+    tiles = jnp.moveaxis(tiles, 0, dim)
+    shape = tiles.shape
+    return tiles.reshape(*shape[:dim], shape[dim] * shape[dim + 1], *shape[dim + 2 :])
+
+
+def ring_gather(x, axis, dim):
+    size = lax.axis_size(axis)
+    pairs = [(i, (i + 1) % size) for i in range(size)]
+    back = [(b, a) for a, b in pairs]
+    lower, upper = ([], [])
+    for lap in range(size - 1):
+        if lap % 2 == 0:
+            lower.append(lax.ppermute(lower[-1] if lower else x, axis, pairs))
+        else:
+            upper.append(lax.ppermute(upper[-1] if upper else x, axis, back))
+    parts = jnp.stack([*lower[::-1], x, *upper])
+    shift = lax.axis_index(axis) - len(lower)
+    parts = parts[(jnp.arange(size) - shift) % size]
+    return laid_out(parts, dim)
 
 
 def silu_parts(gate_sum):
@@ -22,7 +44,7 @@
 
     gate_all, up_all = (
         lax.all_gather(gate_blocks, "narrow", axis=1, tiled=True),
-        lax.all_gather(up_blocks, "narrow", axis=1, tiled=True),
+        ring_gather(up_blocks, "narrow", 1),
     )
     pieces = (gate_all, up_all)
     picked = picks_for()

time: 387 us -> 348 us (0.90)
  waiting for transfers between devices: 234 us -> 164 us
  local copies, waits for them, and re-layouts: 29.3 us -> 46.6 us
  starting transfers between devices: 0.21 us -> 16.8 us
    all_gather x1, waiting for transfers between devices: 47.6 us -> 0.01 us  [shards(): full_inputs = lax.all_gather(inputs, 'wide', axis=1, tiled=True)]
    all_gather x1 -> x0, waiting for transfers between devices: 31 us -> none  [shards(): lax.all_gather(up_blocks, 'narrow', axis=1, tiled=True)]
    ppermute x0 -> x15, waiting for transfers between devices: none -> 27.9 us  [the longest x8 25.6 us: ring_gather(): lower.append(lax.ppermute(lower[-1] if lower else x, axis, pairs))]
    all_gather x1, waiting for transfers between devices: 38.3 us -> 17.8 us  [shards(): lax.all_gather(gate_blocks, 'narrow', axis=1, tiled=True)]
    ppermute x0 -> x15, starting transfers between devices: none -> 16.6 us  [the longest x7 16.6 us: ring_gather(): upper.append(lax.ppermute(upper[-1] if upper else x, axis, back))]
    unnamed x8 -> x28, local copies, waits for them, and re-layouts: 9.13 us -> 20.8 us
    gather x0 -> x1, local copies, waits for them, and re-layouts: none -> 4.93 us  [ring_gather(): parts = parts[(jnp.arange(size) - shift) % size]]
    unnamed x6 -> x5, waiting for transfers between devices: 34.2 us -> 34.7 us
  transfers between devices with their start and end apart: 5 -> 19, of which waited for: 5 -> 15; matrix products, arithmetic and copies ran while one was open for 31% -> 38% of each run, Pallas kernels for 0% -> 0%
where the time goes in v1:
time: 348 us; the launch traced here: 345 us
  waiting for transfers between devices  164 us (47%)
  matrix products  56.4 us (16%)
  other arithmetic  47.8 us (14%)
  local copies, waits for them, and re-layouts  46.6 us (13%)
  starting transfers between devices  16.8 us (5%)
  between operations  13.9 us (4%)
    reduce_scatter x1, waiting for transfers between devices, shards(): lax.psum_scatter(partial_inputs.reshape(tokens_here, row_blocks * block_s...  83.3 us
    scatter-add x16, other arithmetic, one_slot(): return running.at[:, targets].add(contribution)  42.4 us
    unnamed x5, waiting for transfers between devices  34.7 us
    ppermute x8, waiting for transfers between devices, ring_gather(): lower.append(lax.ppermute(lower[-1] if lower else x, axis, pairs))  25.6 us
    unnamed x28, local copies, waits for them, and re-layouts  20.8 us
    dot_general x16, matrix products, one_slot(): jnp.einsum('tjc,jbc->tjb', d_gate, gate_slot, preferred_element_type=jnp....  20 us
    dot_general x16, matrix products, one_slot(): jnp.einsum('tjc,jbc->tjb', d_up, up_slot, preferred_element_type=jnp.floa...  19.7 us
    all_gather x1, waiting for transfers between devices, shards(): lax.all_gather(gate_blocks, 'narrow', axis=1, tiled=True)  17.8 us
  transfers between devices with their start and end apart: 19, of which 15 were waited for; matrix products, arithmetic and copies ran while one was open for 38% of the time, Pallas kernels for 0%

profile of v1, /device:TPU:32, one launch (start us, length us, event | category | flops | bytes accessed | tf_op | source)
XLA Modules:
  0.0 345.2 jit_solution(16476054038144201564)
XLA Ops:
  7.2 1.7 copy.63
  9.0 1.8 copy.66
  10.9 5.6 %collective-permute-done = bf16[7,1,128,128]{3,2,1,0:T(8,128)(2,1)S(1)} collective-permute-done((bf16[7,1,128,128]{3,2,1,0:T(8,128)(2,1)}, bf16[7,1,128,128]{3,2,1,0:T(8,128)(2,1)S(1)}, u32[]{:S(2)}, u32[]{:S(2)}) %collective-permute-start) | collective-permute-done | bytes 229408 | tf_op jit(solution)/shard_map/ppermute | solution.py:20
  16.5 1.7 collective-permute-start.8
  18.3 3.7 %collective-permute-done.1 = bf16[7,1,128,128]{3,2,0,1:T(8,128)(2,1)S(1)} collective-permute-done((bf16[7,1,128,128]{3,2,0,1:T(8,128)(2,1)S(1)}, bf16[7,1,128,128]{3,2,0,1:T(8,128)(2,1)S(1)}, u32[]{:S(2)}, u32[]{:S(2)}) %collective-permute-start.1) | collective-permute-done | bytes 229408 | tf_op jit(solution)/shard_map/ppermute | solution.py:20
  22.1 2.1 collective-permute-start.9
  24.2 3.2 collective-permute-done.2
  27.8 2.2 collective-permute-start.10
  30.0 2.9 collective-permute-done.3
  33.5 2.3 collective-permute-start.11
  35.8 2.5 collective-permute-done.4
  39.4 2.2 collective-permute-start.12
  41.6 3.3 collective-permute-done.5
  45.8 3.0 collective-permute-start.13
  48.7 3.0 collective-permute-done.6
  54.3 3.0 collective-permute-start.14
  57.3 1.5 collective-permute-done.7
  58.7 1.6 bitcast_dynamic-update-slice_fusion.15
  60.4 1.6 bitcast_dynamic-update-slice_fusion.14
  72.0 4.9 %gather_fusion = bf16[16,7,128,128]{3,2,1,0:T(8,128)(2,1)} fusion(bf16[16,7,128,128]{3,2,1,0:T(8,128)(2,1)} %bitcast.29, s32[1024]{0:T(1024)S(1)} %pad_clamp_fusion), kind=kCustom, calls=%fused_computation.1 | custom fusion | bytes 7340096 | tf_op jit(solution)/shard_map/gather | solution.py:25
  76.9 3.2 copy.64
  80.1 2.9 gather_fusion.1
  83.1 6.1 %copy.65 = bf16[7,16,128,128]{2,3,1,0:T(8,128)(2,1)} copy(bf16[7,16,128,128]{3,2,1,0:T(8,128)(2,1)} %bitcast.129) | data formatting | bytes 7340032 | tf_op jit(solution)/shard_map/jit(_take)/gather | solution.py:43
  89.1 17.8 %all-gather.5.cloned.1.call-done = bf16[7,16,128,128]{2,3,1,0:T(8,128)(2,1)} async-done(((bf16[7,1,128,128]{2,3,1,0:T(8,128)(2,1)}), bf16[7,16,128,128]{2,3,1,0:T(8,128)(2,1)}) %all-gather.5.cloned.1.call-update) | async-done | bytes 3670032 | tf_op jit(solution)/shard_map/all_gather | solution.py:46
  106.9 4.5 %convolution_bitcast_fusion = f32[128,7,128]{0,2,1:T(8,128)S(1)} fusion(bf16[7,16,128,128]{2,3,1,0:T(8,128)(2,1)} %all-gather.5.cloned.1.call-done, bf16[7,16,128,128]{2,3,1,0:T(8,128)(2,1)} %copy.65, pred[7,16]{1,0:T(8,128)(4,1)S(1)} %compare_and_fusion), kind=kOutput, calls=%fused_computation.23 | convolution fusion | flops 471597056 | bytes 7798896 | tf_op jit(solution)/shard_map/tjkb,jkbc->tjc/dot_general | solution.py:51
  112.2 2.0 multiply_convert_fusion
  114.4 5.1 %convolution_convert_fusion.1 = bf16[7,16,128,128]{3,2,1,0:T(8,128)(2,1)} fusion(bf16[128,7,128]{0,2,1:T(8,128)(2,1)S(1)} %get-tuple-element.191, bf16[7,16,128,128]{2,3,1,0:T(8,128)(2,1)} %copy.65, pred[7,16]{1,0:T(8,128)(4,1)S(1)} %compare_and_fusion), kind=kOutput, calls=%fused_computation.19 | convolution fusion | flops 473432064 | bytes 7569520 | tf_op jit(solution)/shard_map/tjkb,tjc->jkbc/dot_general | solution.py:83
  119.7 5.0 %convolution_convert_fusion = bf16[7,16,128,128]{3,2,1,0:T(8,128)(2,1)} fusion(bf16[128,7,128]{0,2,1:T(8,128)(2,1)S(1)} %get-tuple-element.190, bf16[7,16,128,128]{2,3,1,0:T(8,128)(2,1)} %copy.65, pred[7,16]{1,0:T(8,128)(4,1)S(1)} %compare_and_fusion), kind=kOutput, calls=%fused_computation.18 | convolution fusion | flops 473432064 | bytes 7569520 | tf_op jit(solution)/shard_map/tjkb,tjc->jkbc/dot_general | solution.py:86
  124.8 2.5 broadcast_in_dim.16
  127.2 85.5 %while.13 = (s32[]{:T(128)}, f32[128,64,128]{2,0,1:T(8,128)}, s32[7,16]{0,1:T(8,128)S(1)}, bf16[7,16,128,128]{2,3,1,0:T(8,128)(2,1)}, bf16[128,7,128]{2,0,1:T(8,...) while((s32[]{:T(128)}, f32[128,64,128]{2,0,1:T(8,128)}, ...), condition=%wide.region_2.4_spmd, body=%wide.region_0.3_spmd.sunk | while | flops 58949656 | bytes 4587709 | solution.py:75
  127.3 1.2 fusion.38
  129.9 2.6 scatter_fusion
  132.6 1.2 fusion.38
  133.8 1.3 fusion.39
  135.3 2.7 scatter_fusion
  138.0 1.3 fusion.38
  140.6 2.7 scatter_fusion
  143.3 1.3 fusion.38
  146.0 2.7 scatter_fusion
  148.7 1.2 fusion.38
  151.3 2.7 scatter_fusion
  154.0 1.3 fusion.38
  156.7 2.6 scatter_fusion
  159.3 1.3 fusion.38
  162.0 2.6 scatter_fusion
  164.7 1.3 fusion.38
  167.4 2.7 scatter_fusion
  170.0 1.2 fusion.38
  172.7 2.7 scatter_fusion
  175.4 1.3 fusion.38
  178.1 2.6 scatter_fusion
  180.7 1.3 fusion.38
  183.4 2.6 scatter_fusion
  188.7 2.6 scatter_fusion
  194.1 2.6 scatter_fusion
  199.4 2.6 scatter_fusion
  202.0 1.3 fusion.38
  204.8 2.7 scatter_fusion
  207.4 1.2 fusion.38
  210.1 2.6 scatter_fusion
  212.7 3.9 %copy_bitcast_fusion = bf16[128,8192]{1,0:T(8,128)(2,1)} fusion(f32[128,64,128]{2,0,1:T(8,128)} %get-tuple-element.129), kind=kLoop, calls=%fused_computation.20 | loop fusion | flops 1048576 | bytes 6291456 | tf_op jit(solution)/shard_map/convert_element_type | solution.py:77
  218.2 34.6 %all-reduce.5.cloned.1.call-done = (bf16[7,16,128,128]{3,2,1,0:T(8,128)(2,1)}, bf16[7,16,128,128]{3,2,1,0:T(8,128)(2,1)}) async-done(((bf16[7,16,128,128]{3,2,1,0:T(8,128)(2,1)}, bf16[7,16,128,128]{3,2,1,0:T(8,128)(2,1)}), (bf16[7,16,128,128]{3,2,1,0:T(8,128)(2,1)}, bf16[7,16,128,128]{3,2,1,0:T(8,128)(2,1)})) %all-reduce.5.cloned.1.call-update) | async-done | bytes 7340048
  252.8 2.5 constant_dynamic-slice_fusion.1
  255.4 83.3 %reduce-scatter.8.cloned.1.call-done = bf16[128,512]{1,0:T(8,128)(2,1)} async-done(((bf16[128,8192]{1,0:T(8,128)(2,1)}), bf16[128,512]{1,0:T(8,128)(2,1)}) %reduce-scatter.8.cloned.1.call-update) | async-done | bytes 131088 | tf_op jit(solution)/shard_map/reduce_scatter | solution.py:76
  (108 shorter events, 43.9 us)
Async XLA Ops:
  7.2 59.1 %copy-start.2 = (bf16[7,1,128,128]{3,2,1,0:T(8,128)(2,1)S(1)}, bf16[7,1,128,128]{3,2,1,0:T(8,128)(2,1)}, u32[]{:S(2)}) copy-start(bf16[7,1,128,128]{3,2,1,0:T(8,128)(2,1)} %param.11) | copy-start | bytes 688132
  7.2 69.7 %all-gather.3.cloned.1.call-start = ((), (), s32[]{:S(2)}) async-start(), calls=%async_computation.1 | async-start | bytes 2228224 | tf_op jit(solution)/shard_map/all_gather | solution.py:38
  9.0 98.0 %all-gather.5.cloned.1.call-start = ((), (), s32[]{:S(2)}) async-start(), calls=%async_computation.2 | async-start | bytes 3899392 | tf_op jit(solution)/shard_map/all_gather | solution.py:46
  10.8 242.0 %all-reduce.5.cloned.1.call-start = ((), (), s32[]{:S(2)}) async-start(), calls=%async_computation.4 | async-start | bytes 14680064
  10.9 5.7 %collective-permute-start = (bf16[7,1,128,128]{3,2,1,0:T(8,128)(2,1)}, bf16[7,1,128,128]{3,2,1,0:T(8,128)(2,1)S(1)}, u32[]{:S(2)}, u32[]{:S(2)}) collective-permute-start(bf16[7,1,128,128]{3,2,1,0:T(8,128)(2,1)} %param.11), channel_id=1, source_target_pairs={{0,16},{16,32},{32,48},{48,64},{64,80},{80,96},{96,112},{112,128},... | collective-permute-start | bytes 688136 | tf_op jit(solution)/shard_map/ppermute | solution.py:20
  16.5 5.4 %collective-permute-start.1 = (bf16[7,1,128,128]{3,2,0,1:T(8,128)(2,1)S(1)}, bf16[7,1,128,128]{3,2,0,1:T(8,128)(2,1)S(1)}, u32[]{:S(2)}, u32[]{:S(2)}) collective-permute-start(bf16[7,1,128,128]{3,2,0,1:T(8,128)(2,1)S(1)} %bitcast.134), channel_id=1, source_target_pairs={{0,16},{16,32},{32,48},{48,64},{64,80},{80,96},{96,112},{112,128},... | collective-permute-start | bytes 688136 | tf_op jit(solution)/shard_map/ppermute | solution.py:20
  16.5 5.6 %collective-permute-start.8 = (bf16[7,1,128,128]{3,2,0,1:T(8,128)(2,1)}, bf16[7,1,128,128]{3,2,0,1:T(8,128)(2,1)S(1)}, u32[]{:S(2)}, u32[]{:S(2)}) collective-permute-start(bf16[7,1,128,128]{3,2,0,1:T(8,128)(2,1)} %bitcast.133), channel_id=1, source_target_pairs={{16,0},{32,16},{48,32},{64,48},{80,64},{96,80},{112,96},{128,112},... | collective-permute-start | bytes 688136 | tf_op jit(solution)/shard_map/ppermute | solution.py:22
  22.0 5.4 %collective-permute-start.2 = (bf16[7,1,128,128]{3,2,0,1:T(8,128)(2,1)S(1)}, bf16[7,1,128,128]{3,2,0,1:T(8,128)(2,1)S(1)}, u32[]{:S(2)}, u32[]{:S(2)}) collective-permute-start(bf16[7,1,128,128]{3,2,0,1:T(8,128)(2,1)S(1)} %collective-permute-done.1), channel_id=1, source_target_pairs={{0,16},{16,32},{32,48},{48,64},{64,80},{80,96},{96,112},{112,128},... | collective-permute-start | bytes 688136 | tf_op jit(solution)/shard_map/ppermute | solution.py:20
  22.1 5.6 %collective-permute-start.9 = (bf16[7,1,128,128]{3,2,0,1:T(8,128)(2,1)S(1)}, bf16[7,1,128,128]{3,2,0,1:T(8,128)(2,1)S(1)}, u32[]{:S(2)}, u32[]{:S(2)}) collective-permute-start(bf16[7,1,128,128]{3,2,0,1:T(8,128)(2,1)S(1)} %collective-permute-done.8), channel_id=1, source_target_pairs={{16,0},{32,16},{48,32},{64,48},{80,64},{96,80},{112,96},{128,112},... | collective-permute-start | bytes 688136 | tf_op jit(solution)/shard_map/ppermute | solution.py:22
  27.4 5.4 %collective-permute-start.3 = (bf16[7,1,128,128]{3,2,0,1:T(8,128)(2,1)S(1)}, bf16[7,1,128,128]{3,2,0,1:T(8,128)(2,1)S(1)}, u32[]{:S(2)}, u32[]{:S(2)}) collective-permute-start(bf16[7,1,128,128]{3,2,0,1:T(8,128)(2,1)S(1)} %collective-permute-done.2), channel_id=1, source_target_pairs={{0,16},{16,32},{32,48},{48,64},{64,80},{80,96},{96,112},{112,128},... | collective-permute-start | bytes 688136 | tf_op jit(solution)/shard_map/ppermute | solution.py:20
  27.8 5.8 %collective-permute-start.10 = (bf16[7,1,128,128]{3,2,0,1:T(8,128)(2,1)S(1)}, bf16[7,1,128,128]{3,2,0,1:T(8,128)(2,1)S(1)}, u32[]{:S(2)}, u32[]{:S(2)}) collective-permute-start(bf16[7,1,128,128]{3,2,0,1:T(8,128)(2,1)S(1)} %collective-permute-done.9), channel_id=1, source_target_pairs={{16,0},{32,16},{48,32},{64,48},{80,64},{96,80},{112,96},{128,112},... | collective-permute-start | bytes 688136 | tf_op jit(solution)/shard_map/ppermute | solution.py:22
  32.9 5.4 %collective-permute-start.4 = (bf16[7,1,128,128]{3,2,0,1:T(8,128)(2,1)S(1)}, bf16[7,1,128,128]{3,2,0,1:T(8,128)(2,1)S(1)}, u32[]{:S(2)}, u32[]{:S(2)}) collective-permute-start(bf16[7,1,128,128]{3,2,0,1:T(8,128)(2,1)S(1)} %collective-permute-done.3), channel_id=1, source_target_pairs={{0,16},{16,32},{32,48},{48,64},{64,80},{80,96},{96,112},{112,128},... | collective-permute-start | bytes 688136 | tf_op jit(solution)/shard_map/ppermute | solution.py:20
  33.5 5.8 %collective-permute-start.11 = (bf16[7,1,128,128]{3,2,0,1:T(8,128)(2,1)S(1)}, bf16[7,1,128,128]{3,2,0,1:T(8,128)(2,1)S(1)}, u32[]{:S(2)}, u32[]{:S(2)}) collective-permute-start(bf16[7,1,128,128]{3,2,0,1:T(8,128)(2,1)S(1)} %collective-permute-done.10), channel_id=1, source_target_pairs={{16,0},{32,16},{48,32},{64,48},{80,64},{96,80},{112,96},{128,112},... | collective-permute-start | bytes 688136 | tf_op jit(solution)/shard_map/ppermute | solution.py:22
  38.3 6.7 %collective-permute-start.5 = (bf16[7,1,128,128]{3,2,0,1:T(8,128)(2,1)S(1)}, bf16[7,1,128,128]{3,2,0,1:T(8,128)(2,1)S(1)}, u32[]{:S(2)}, u32[]{:S(2)}) collective-permute-start(bf16[7,1,128,128]{3,2,0,1:T(8,128)(2,1)S(1)} %collective-permute-done.4), channel_id=1, source_target_pairs={{0,16},{16,32},{32,48},{48,64},{64,80},{80,96},{96,112},{112,128},... | collective-permute-start | bytes 688136 | tf_op jit(solution)/shard_map/ppermute | solution.py:20
  39.4 6.4 %collective-permute-start.12 = (bf16[7,1,128,128]{3,2,0,1:T(8,128)(2,1)S(1)}, bf16[7,1,128,128]{3,2,0,1:T(8,128)(2,1)S(1)}, u32[]{:S(2)}, u32[]{:S(2)}) collective-permute-start(bf16[7,1,128,128]{3,2,0,1:T(8,128)(2,1)S(1)} %collective-permute-done.11), channel_id=1, source_target_pairs={{16,0},{32,16},{48,32},{64,48},{80,64},{96,80},{112,96},{128,112},... | collective-permute-start | bytes 688136 | tf_op jit(solution)/shard_map/ppermute | solution.py:22
  45.0 6.8 %collective-permute-start.6 = (bf16[7,1,128,128]{3,2,0,1:T(8,128)(2,1)S(1)}, bf16[7,1,128,128]{3,2,0,1:T(8,128)(2,1)}, u32[]{:S(2)}, u32[]{:S(2)}) collective-permute-start(bf16[7,1,128,128]{3,2,0,1:T(8,128)(2,1)S(1)} %collective-permute-done.5), channel_id=1, source_target_pairs={{0,16},{16,32},{32,48},{48,64},{64,80},{80,96},{96,112},{112,128},... | collective-permute-start | bytes 688136 | tf_op jit(solution)/shard_map/ppermute | solution.py:20
  45.8 8.5 %collective-permute-start.13 = (bf16[7,1,128,128]{3,2,0,1:T(8,128)(2,1)S(1)}, bf16[7,1,128,128]{3,2,0,1:T(8,128)(2,1)S(1)}, u32[]{:S(2)}, u32[]{:S(2)}) collective-permute-start(bf16[7,1,128,128]{3,2,0,1:T(8,128)(2,1)S(1)} %collective-permute-done.12), channel_id=1, source_target_pairs={{16,0},{32,16},{48,32},{64,48},{80,64},{96,80},{112,96},{128,112},... | collective-permute-start | bytes 688136 | tf_op jit(solution)/shard_map/ppermute | solution.py:22
  51.7 7.0 %collective-permute-start.7 = (bf16[7,1,128,128]{3,2,0,1:T(8,128)(2,1)}, bf16[7,1,128,128]{3,2,0,1:T(8,128)(2,1)}, u32[]{:S(2)}, u32[]{:S(2)}) collective-permute-start(bf16[7,1,128,128]{3,2,0,1:T(8,128)(2,1)} %collective-permute-done.6), channel_id=1, source_target_pairs={{0,16},{16,32},{32,48},{48,64},{64,80},{80,96},{96,112},{112,128},... | collective-permute-start | bytes 688136 | tf_op jit(solution)/shard_map/ppermute | solution.py:20
  54.3 17.0 %collective-permute-start.14 = (bf16[7,1,128,128]{3,2,0,1:T(8,128)(2,1)S(1)}, bf16[7,1,128,128]{3,2,0,1:T(8,128)(2,1)S(1)}, u32[]{:S(2)}, u32[]{:S(2)}) collective-permute-start(bf16[7,1,128,128]{3,2,0,1:T(8,128)(2,1)S(1)} %collective-permute-done.13), channel_id=1, source_target_pairs={{16,0},{32,16},{48,32},{64,48},{80,64},{96,80},{112,96},{128,112},... | collective-permute-start | bytes 688136 | tf_op jit(solution)/shard_map/ppermute | solution.py:22
  106.9 4.5 %copy-start = (bf16[16,7,128,128]{3,2,1,0:T(8,128)(2,1)S(1)}, bf16[16,7,128,128]{3,2,1,0:T(8,128)(2,1)}, u32[]{:S(2)}) copy-start(bf16[16,7,128,128]{3,2,1,0:T(8,128)(2,1)} %gather_fusion) | copy-start | bytes 11010052
  106.9 5.3 %copy-start.1 = (bf16[7,16,128,128]{2,3,1,0:T(8,128)(2,1)S(1)}, bf16[7,16,128,128]{2,3,1,0:T(8,128)(2,1)}, u32[]{:S(2)}) copy-start(bf16[7,16,128,128]{2,3,1,0:T(8,128)(2,1)} %copy.65) | copy-start | bytes 11010052
  124.7 213.9 %reduce-scatter.8.cloned.1.call-start = ((), (), s32[]{:S(2)}) async-start(), calls=%async_computation.3 | async-start | bytes 2228224 | tf_op jit(solution)/shard_map/reduce_scatter | solution.py:76
  212.7 4.0 %copy-start.3 = (u32[256]{0:T(256)S(1)}, u32[256]{0:T(256)}, u32[]{:S(2)}) copy-start(u32[256]{0:T(256)} %constant.82) | copy-start | bytes 3076
Sparse Core Ops, SparseCore 0:
  11.0 52.5 all-gather.2
  66.0 40.8 all-gather.4
  124.8 127.9 all-reduce.4
  256.8 81.7 reduce-scatter.7
